TPU v7x, 32 devices: a whole 2x2x4 slice. The times are simulated.
32 devices in a mesh: mesh: 8 (over y, x, core), band: 4 (over z).
Axes of the slice: x: 2, y: 2, z: 4, core: 2. Of those that a mesh axis runs over, the one named last changes fastest.
Arguments:
- states: float32 [2, 64, 8192], P(None, 'band', 'mesh'), may hold values from -6 to 6
- frozen: float32 [2, 32, 8192], P(None, 'band', 'mesh'), may hold values from -0.125 to 0.125
- weights: float32 [8, 8192], P(None, 'mesh'), may hold values from 0.1 to 1
- potential: float32 [8192], P('mesh'), may hold values from -2 to 2
- send_list: int32 [8, 8, 256], P('mesh'), may hold values from 0 to 1023
- neighbours: int32 [8, 8192], P(None, 'mesh'), may hold values from 0 to 3071, as said below
Outputs:
- evolved: float32 [2, 64, 8192], P(None, 'band', 'mesh')
Inputs may be any that keep to these rules, and one draw needn't show every extreme that they name: `neighbours`: an entry below 1024 names a point of the same part; an entry 1024 + s * 256 + c names ghost slot c from part s, where part s is at most 3 parts away in the cyclic order of parts or exactly half the number of parts away, and every part names ghost slots from all those parts. Slots of send_list[s, i] that part i never names hold arbitrary points of part s.
All inputs are finite; a program needn't handle non-finite values.
Results may differ from a plain program's by a relative error of at most 0.0001.
Values sent between devices are 32-bit elements; how exact they have to be, the bound alone decides.
No kernel may reach another device: no remote copies, remote signals or barrier semaphores. Data moves between devices by JAX's collectives and lax.ppermute only.
A program may use at most 128 MiB of HBM per device.

v0:
```python
import jax
import jax.numpy as jnp
from jax import lax
from jax.sharding import PartitionSpec as P

NBRS = 8
TERMS = 4
time_step = 0.3


def rotate(field):
    return jnp.stack([field[1], -field[0]])


def body(states, frozen, weights, potential, send_list, neighbours):
    parts = lax.axis_size("mesh")
    rows = states.shape[1]
    capacity = send_list.shape[2]
    routes = send_list[0]
    full_frozen = lax.all_gather(frozen, "band", axis=1, tiled=True)
    total = states
    term = states
    for order in range(1, TERMS + 1):
        paired = jnp.stack([term, rotate(term)])
        partial_intersection = jnp.einsum(
            "cmp,ocjp->omj", full_frozen, paired, precision=lax.Precision.HIGHEST
        )
        intersection = lax.psum(partial_intersection, "mesh")
        packed = jnp.take(term, routes.reshape(-1), axis=2).reshape(2, rows, parts, capacity)
        arrived = lax.all_to_all(packed, "mesh", split_axis=2, concat_axis=2, tiled=True)
        extended = jnp.concatenate([term, arrived.reshape(2, rows, parts * capacity)], axis=2)
        stencil = jnp.zeros_like(term)
        for apply_order in range(NBRS):
            stencil = stencil + weights[apply_order] * (
                jnp.take(extended, neighbours[apply_order], axis=2) - term
            )
        blocks = jnp.stack(
            [
                jnp.stack([intersection[0], -intersection[1]]),
                jnp.stack([intersection[1], intersection[0]]),
            ]
        )
        exchange = jnp.einsum("dmp,cdmj->cjp", full_frozen, blocks, precision=lax.Precision.HIGHEST)
        image = -0.5 * stencil + potential * term - exchange
        term = time_step / order * rotate(image)
        total = total + term
    return total


def solution(mesh):
    return jax.shard_map(
        body,
        mesh=mesh,
        in_specs=(
            P(None, "band", "mesh"),
            P(None, "band", "mesh"),
            P(None, "mesh"),
            P("mesh"),
            P("mesh", None, None),
            P(None, "mesh"),
        ),
        out_specs=P(None, "band", "mesh"),
        check_vma=False,
    )
```

profile of v0, /device:TPU:0, one launch (start us, length us, event | category | flops | bytes accessed | tf_op | source)
XLA Modules:
  0.0 581.9 jit_solution(13586005560089532101)
XLA Ops:
  2.1 14.4 %gather_fusion = f32[2048,2,16]{2,1,0:T(2,128)} fusion(f32[2,16,1024]{1,0,2:T(2,128)S(1)} %copy.119, s32[2048]{0:T(1024)S(1)} %fusion.108), kind=kCustom, calls=%fused_computation.clone | custom fusion | bytes 532480 | tf_op jit(solution)/shard_map/jit(_take)/gather | solution.py:29
  16.5 10.0 %broadcast_select_fusion.3 = f32[2048,2,16]{2,1,0:T(2,128)S(1)} fusion(f32[2048,2,16]{2,1,0:T(2,128)} %gather_fusion, pred[2048]{0:T(1024)(128)(4,1)S(1)} %compare_and_fusion), kind=kLoop, calls=%fused_computation.39 | loop fusion | flops 65536 | bytes 526336 | tf_op jit(solution)/shard_map/jit(_take)/select_n | solution.py:29
  39.6 14.2 %all_gather.3 = f32[2,32,1024]{2,1,0:T(8,128)S(1)} all-gather(f32[2,8,1024]{2,1,0:T(8,128)S(1)} %copy-done.34), channel_id=1, replica_groups=mesh['mesh'=8,'band'=4] {'band'}, dimensions={1}, use_global_device_ids=true | all-gather | bytes 327680 | tf_op jit(solution)/shard_map/all_gather | solution.py:20
  54.3 23.0 %psum.28 = f32[2,32,16]{1,2,0:T(8,128)S(1)} all-reduce(f32[2,32,16]{1,2,0:T(8,128)S(1)} %convolution_bitcast_fusion.7), channel_id=1, replica_groups=mesh['mesh'=8,'band'=4] {'mesh'}, use_global_device_ids=true, to_apply=%region_0.3 | all-reduce | flops 1024 | bytes 8192 | tf_op jit(solution)/shard_map/psum | solution.py:28
  84.0 7.6 %gather_fusion.1 = f32[1024,2,16]{2,1,0:T(2,128)} fusion(f32[2,16,3072]{1,0,2:T(2,128)S(1)} %copy.122, s32[1024]{0:T(1024)} %fusion.109), kind=kCustom, calls=%fused_computation.1.clone | custom fusion | bytes 266240 | tf_op jit(solution)/shard_map/jit(_take)/gather | solution.py:35
  93.7 7.6 %gather_fusion.2 = f32[1024,2,16]{2,1,0:T(2,128)} fusion(f32[2,16,3072]{1,0,2:T(2,128)S(1)} %copy.122, s32[1024]{0:T(1024)} %fusion.110), kind=kCustom, calls=%fused_computation.5.clone | custom fusion | bytes 266240 | tf_op jit(solution)/shard_map/jit(_take)/gather | solution.py:35
  103.3 7.6 %gather_fusion.3 = f32[1024,2,16]{2,1,0:T(2,128)} fusion(f32[2,16,3072]{1,0,2:T(2,128)S(1)} %copy.122, s32[1024]{0:T(1024)} %fusion.111), kind=kCustom, calls=%fused_computation.6.clone | custom fusion | bytes 266240 | tf_op jit(solution)/shard_map/jit(_take)/gather | solution.py:35
  112.9 7.6 %gather_fusion.4 = f32[1024,2,16]{2,1,0:T(2,128)} fusion(f32[2,16,3072]{1,0,2:T(2,128)S(1)} %copy.122, s32[1024]{0:T(1024)} %fusion.112), kind=kCustom, calls=%fused_computation.7.clone | custom fusion | bytes 266240 | tf_op jit(solution)/shard_map/jit(_take)/gather | solution.py:35
  122.5 7.6 %gather_fusion.5 = f32[1024,2,16]{2,1,0:T(2,128)} fusion(f32[2,16,3072]{1,0,2:T(2,128)S(1)} %copy.122, s32[1024]{0:T(1024)} %fusion.113), kind=kCustom, calls=%fused_computation.8.clone | custom fusion | bytes 266240 | tf_op jit(solution)/shard_map/jit(_take)/gather | solution.py:35
  132.1 7.6 %gather_fusion.6 = f32[1024,2,16]{2,1,0:T(2,128)} fusion(f32[2,16,3072]{1,0,2:T(2,128)S(1)} %copy.122, s32[1024]{0:T(1024)} %fusion.114), kind=kCustom, calls=%fused_computation.9.clone | custom fusion | bytes 266240 | tf_op jit(solution)/shard_map/jit(_take)/gather | solution.py:35
  141.7 7.5 %gather_fusion.7 = f32[1024,2,16]{2,1,0:T(2,128)} fusion(f32[2,16,3072]{1,0,2:T(2,128)S(1)} %copy.122, s32[1024]{0:T(1024)S(1)} %fusion.115), kind=kCustom, calls=%fused_computation.10.clone | custom fusion | bytes 266240 | tf_op jit(solution)/shard_map/jit(_take)/gather | solution.py:35
  151.2 7.5 %gather_fusion.8 = f32[1024,2,16]{2,1,0:T(2,128)} fusion(f32[2,16,3072]{1,0,2:T(2,128)S(1)} %copy.122, s32[1024]{0:T(1024)S(1)} %fusion.116), kind=kCustom, calls=%fused_computation.11.clone | custom fusion | bytes 266240 | tf_op jit(solution)/shard_map/jit(_take)/gather | solution.py:35
  163.5 22.3 %psum.29 = f32[2,32,16]{1,2,0:T(8,128)S(1)} all-reduce(f32[2,32,16]{1,2,0:T(8,128)S(1)} %convolution_bitcast_fusion.6), channel_id=1, replica_groups=mesh['mesh'=8,'band'=4] {'mesh'}, use_global_device_ids=true, to_apply=%region_1.4 | all-reduce | flops 1024 | bytes 8192 | tf_op jit(solution)/shard_map/psum | solution.py:28
  185.8 14.4 %gather_fusion.9 = f32[2048,2,16]{2,1,0:T(2,128)} fusion(f32[2,16,1024]{1,0,2:T(2,128)S(1)} %copy.138, s32[2048]{0:T(1024)S(1)} %fusion.108), kind=kCustom, calls=%fused_computation.2.clone | custom fusion | bytes 532480 | tf_op jit(solution)/shard_map/jit(_take)/gather | solution.py:29
  200.2 10.0 %broadcast_select_fusion.2 = f32[2048,2,16]{2,1,0:T(2,128)S(1)} fusion(f32[2048,2,16]{2,1,0:T(2,128)} %gather_fusion.9, pred[2048]{0:T(1024)(128)(4,1)S(1)} %copy-done.36), kind=kLoop, calls=%fused_computation.38 | loop fusion | flops 65536 | bytes 526336 | tf_op jit(solution)/shard_map/jit(_take)/select_n | solution.py:29
  216.3 6.1 %all-to-all-done.1 = f32[2,16,8,256]{3,1,0,2:T(8,128)S(1)} async-done(((f32[2,16,8,256]{3,1,0,2:T(8,128)}), f32[2,16,8,256]{3,1,0,2:T(8,128)S(1)}, u32[]{:S(2)}, u32[]{:S(2)}) %all-to-all-start.1) | async-done | bytes 262176 | tf_op jit(solution)/shard_map/all_to_all | solution.py:30
  227.3 7.6 %gather_fusion.10 = f32[1024,2,16]{2,1,0:T(2,128)} fusion(f32[2,16,3072]{1,0,2:T(2,128)S(1)} %copy.141, s32[1024]{0:T(1024)} %fusion.109), kind=kCustom, calls=%fused_computation.12.clone | custom fusion | bytes 266240 | tf_op jit(solution)/shard_map/jit(_take)/gather | solution.py:35
  235.0 7.6 %gather_fusion.11 = f32[1024,2,16]{2,1,0:T(2,128)} fusion(f32[2,16,3072]{1,0,2:T(2,128)S(1)} %copy.141, s32[1024]{0:T(1024)} %fusion.110), kind=kCustom, calls=%fused_computation.13.clone | custom fusion | bytes 266240 | tf_op jit(solution)/shard_map/jit(_take)/gather | solution.py:35
  242.6 7.6 %gather_fusion.12 = f32[1024,2,16]{2,1,0:T(2,128)} fusion(f32[2,16,3072]{1,0,2:T(2,128)S(1)} %copy.141, s32[1024]{0:T(1024)} %fusion.111), kind=kCustom, calls=%fused_computation.14.clone | custom fusion | bytes 266240 | tf_op jit(solution)/shard_map/jit(_take)/gather | solution.py:35
  250.2 7.6 %gather_fusion.13 = f32[1024,2,16]{2,1,0:T(2,128)} fusion(f32[2,16,3072]{1,0,2:T(2,128)S(1)} %copy.141, s32[1024]{0:T(1024)} %fusion.112), kind=kCustom, calls=%fused_computation.15.clone | custom fusion | bytes 266240 | tf_op jit(solution)/shard_map/jit(_take)/gather | solution.py:35
  257.8 7.6 %gather_fusion.14 = f32[1024,2,16]{2,1,0:T(2,128)} fusion(f32[2,16,3072]{1,0,2:T(2,128)S(1)} %copy.141, s32[1024]{0:T(1024)} %fusion.113), kind=kCustom, calls=%fused_computation.16.clone | custom fusion | bytes 266240 | tf_op jit(solution)/shard_map/jit(_take)/gather | solution.py:35
  265.4 7.6 %gather_fusion.15 = f32[1024,2,16]{2,1,0:T(2,128)} fusion(f32[2,16,3072]{1,0,2:T(2,128)S(1)} %copy.141, s32[1024]{0:T(1024)} %fusion.114), kind=kCustom, calls=%fused_computation.17.clone | custom fusion | bytes 266240 | tf_op jit(solution)/shard_map/jit(_take)/gather | solution.py:35
  273.0 7.5 %gather_fusion.16 = f32[1024,2,16]{2,1,0:T(2,128)} fusion(f32[2,16,3072]{1,0,2:T(2,128)S(1)} %copy.141, s32[1024]{0:T(1024)S(1)} %fusion.115), kind=kCustom, calls=%fused_computation.18.clone | custom fusion | bytes 266240 | tf_op jit(solution)/shard_map/jit(_take)/gather | solution.py:35
  280.5 7.5 %gather_fusion.17 = f32[1024,2,16]{2,1,0:T(2,128)} fusion(f32[2,16,3072]{1,0,2:T(2,128)S(1)} %copy.141, s32[1024]{0:T(1024)S(1)} %fusion.116), kind=kCustom, calls=%fused_computation.19.clone | custom fusion | bytes 266240 | tf_op jit(solution)/shard_map/jit(_take)/gather | solution.py:35
  303.7 22.3 %psum.30 = f32[2,32,16]{1,2,0:T(8,128)S(1)} all-reduce(f32[2,32,16]{1,2,0:T(8,128)S(1)} %convolution_bitcast_fusion.5), channel_id=1, replica_groups=mesh['mesh'=8,'band'=4] {'mesh'}, use_global_device_ids=true, to_apply=%region_2.5 | all-reduce | flops 1024 | bytes 8192 | tf_op jit(solution)/shard_map/psum | solution.py:28
  326.0 14.4 %gather_fusion.18 = f32[2048,2,16]{2,1,0:T(2,128)} fusion(f32[2,16,1024]{1,0,2:T(2,128)S(1)} %copy.157, s32[2048]{0:T(1024)S(1)} %fusion.108), kind=kCustom, calls=%fused_computation.3.clone | custom fusion | bytes 532480 | tf_op jit(solution)/shard_map/jit(_take)/gather | solution.py:29
  340.4 10.0 %broadcast_select_fusion.1 = f32[2048,2,16]{2,1,0:T(2,128)S(1)} fusion(f32[2048,2,16]{2,1,0:T(2,128)} %gather_fusion.18, pred[2048]{0:T(1024)(128)(4,1)S(1)} %copy-done.37), kind=kLoop, calls=%fused_computation.37 | loop fusion | flops 65536 | bytes 526336 | tf_op jit(solution)/shard_map/jit(_take)/select_n | solution.py:29
  356.3 6.2 %all-to-all-done.2 = f32[2,16,8,256]{3,1,0,2:T(8,128)S(1)} async-done(((f32[2,16,8,256]{3,1,0,2:T(8,128)}), f32[2,16,8,256]{3,1,0,2:T(8,128)S(1)}, u32[]{:S(2)}, u32[]{:S(2)}) %all-to-all-start.2) | async-done | bytes 262176 | tf_op jit(solution)/shard_map/all_to_all | solution.py:30
  367.5 7.6 %gather_fusion.19 = f32[1024,2,16]{2,1,0:T(2,128)} fusion(f32[2,16,3072]{1,0,2:T(2,128)S(1)} %copy.160, s32[1024]{0:T(1024)} %fusion.109), kind=kCustom, calls=%fused_computation.20.clone | custom fusion | bytes 266240 | tf_op jit(solution)/shard_map/jit(_take)/gather | solution.py:35
  375.2 7.6 %gather_fusion.20 = f32[1024,2,16]{2,1,0:T(2,128)} fusion(f32[2,16,3072]{1,0,2:T(2,128)S(1)} %copy.160, s32[1024]{0:T(1024)} %fusion.110), kind=kCustom, calls=%fused_computation.21.clone | custom fusion | bytes 266240 | tf_op jit(solution)/shard_map/jit(_take)/gather | solution.py:35
  382.8 7.6 %gather_fusion.21 = f32[1024,2,16]{2,1,0:T(2,128)} fusion(f32[2,16,3072]{1,0,2:T(2,128)S(1)} %copy.160, s32[1024]{0:T(1024)} %fusion.111), kind=kCustom, calls=%fused_computation.22.clone | custom fusion | bytes 266240 | tf_op jit(solution)/shard_map/jit(_take)/gather | solution.py:35
  390.4 7.6 %gather_fusion.22 = f32[1024,2,16]{2,1,0:T(2,128)} fusion(f32[2,16,3072]{1,0,2:T(2,128)S(1)} %copy.160, s32[1024]{0:T(1024)} %fusion.112), kind=kCustom, calls=%fused_computation.23.clone | custom fusion | bytes 266240 | tf_op jit(solution)/shard_map/jit(_take)/gather | solution.py:35
  398.0 7.6 %gather_fusion.23 = f32[1024,2,16]{2,1,0:T(2,128)} fusion(f32[2,16,3072]{1,0,2:T(2,128)S(1)} %copy.160, s32[1024]{0:T(1024)} %fusion.113), kind=kCustom, calls=%fused_computation.24.clone | custom fusion | bytes 266240 | tf_op jit(solution)/shard_map/jit(_take)/gather | solution.py:35
  405.6 7.6 %gather_fusion.24 = f32[1024,2,16]{2,1,0:T(2,128)} fusion(f32[2,16,3072]{1,0,2:T(2,128)S(1)} %copy.160, s32[1024]{0:T(1024)} %fusion.114), kind=kCustom, calls=%fused_computation.25.clone | custom fusion | bytes 266240 | tf_op jit(solution)/shard_map/jit(_take)/gather | solution.py:35
  413.2 7.5 %gather_fusion.25 = f32[1024,2,16]{2,1,0:T(2,128)} fusion(f32[2,16,3072]{1,0,2:T(2,128)S(1)} %copy.160, s32[1024]{0:T(1024)S(1)} %fusion.115), kind=kCustom, calls=%fused_computation.26.clone | custom fusion | bytes 266240 | tf_op jit(solution)/shard_map/jit(_take)/gather | solution.py:35
  420.7 7.5 %gather_fusion.26 = f32[1024,2,16]{2,1,0:T(2,128)} fusion(f32[2,16,3072]{1,0,2:T(2,128)S(1)} %copy.160, s32[1024]{0:T(1024)S(1)} %fusion.116), kind=kCustom, calls=%fused_computation.27.clone | custom fusion | bytes 266240 | tf_op jit(solution)/shard_map/jit(_take)/gather | solution.py:35
  443.8 22.3 %psum.31 = f32[2,32,16]{1,2,0:T(8,128)S(1)} all-reduce(f32[2,32,16]{1,2,0:T(8,128)S(1)} %convolution_bitcast_fusion.4), channel_id=1, replica_groups=mesh['mesh'=8,'band'=4] {'mesh'}, use_global_device_ids=true, to_apply=%region_3.6 | all-reduce | flops 1024 | bytes 8192 | tf_op jit(solution)/shard_map/psum | solution.py:28
  466.1 14.4 %gather_fusion.27 = f32[2048,2,16]{2,1,0:T(2,128)} fusion(f32[2,16,1024]{1,0,2:T(2,128)S(1)} %copy.176, s32[2048]{0:T(1024)S(1)} %fusion.108), kind=kCustom, calls=%fused_computation.4.clone | custom fusion | bytes 532480 | tf_op jit(solution)/shard_map/jit(_take)/gather | solution.py:29
  480.6 10.0 %broadcast_select_fusion = f32[2048,2,16]{2,1,0:T(2,128)S(1)} fusion(f32[2048,2,16]{2,1,0:T(2,128)} %gather_fusion.27, pred[2048]{0:T(1024)(128)(4,1)S(1)} %copy-done.38), kind=kLoop, calls=%fused_computation.36 | loop fusion | flops 65536 | bytes 526336 | tf_op jit(solution)/shard_map/jit(_take)/select_n | solution.py:29
  496.8 6.0 %all-to-all-done.3 = f32[2,16,8,256]{3,1,0,2:T(8,128)S(1)} async-done(((f32[2,16,8,256]{3,1,0,2:T(8,128)}), f32[2,16,8,256]{3,1,0,2:T(8,128)S(1)}, u32[]{:S(2)}, u32[]{:S(2)}) %all-to-all-start.3) | async-done | bytes 262176 | tf_op jit(solution)/shard_map/all_to_all | solution.py:30
  507.8 7.6 %gather_fusion.28 = f32[1024,2,16]{2,1,0:T(2,128)} fusion(f32[2,16,3072]{1,0,2:T(2,128)S(1)} %copy.179, s32[1024]{0:T(1024)} %fusion.109), kind=kCustom, calls=%fused_computation.28.clone | custom fusion | bytes 266240 | tf_op jit(solution)/shard_map/jit(_take)/gather | solution.py:35
  515.4 7.6 %gather_fusion.29 = f32[1024,2,16]{2,1,0:T(2,128)} fusion(f32[2,16,3072]{1,0,2:T(2,128)S(1)} %copy.179, s32[1024]{0:T(1024)} %fusion.110), kind=kCustom, calls=%fused_computation.29.clone | custom fusion | bytes 266240 | tf_op jit(solution)/shard_map/jit(_take)/gather | solution.py:35
  523.0 7.6 %gather_fusion.30 = f32[1024,2,16]{2,1,0:T(2,128)} fusion(f32[2,16,3072]{1,0,2:T(2,128)S(1)} %copy.179, s32[1024]{0:T(1024)} %fusion.111), kind=kCustom, calls=%fused_computation.30.clone | custom fusion | bytes 266240 | tf_op jit(solution)/shard_map/jit(_take)/gather | solution.py:35
  530.6 7.6 %gather_fusion.31 = f32[1024,2,16]{2,1,0:T(2,128)} fusion(f32[2,16,3072]{1,0,2:T(2,128)S(1)} %copy.179, s32[1024]{0:T(1024)} %fusion.112), kind=kCustom, calls=%fused_computation.31.clone | custom fusion | bytes 266240 | tf_op jit(solution)/shard_map/jit(_take)/gather | solution.py:35
  538.2 7.5 %gather_fusion.32 = f32[1024,2,16]{2,1,0:T(2,128)} fusion(f32[2,16,3072]{1,0,2:T(2,128)S(1)} %copy.179, s32[1024]{0:T(1024)S(1)} %copy-done.29), kind=kCustom, calls=%fused_computation.32.clone | custom fusion | bytes 266240 | tf_op jit(solution)/shard_map/jit(_take)/gather | solution.py:35
  545.7 7.5 %gather_fusion.33 = f32[1024,2,16]{2,1,0:T(2,128)} fusion(f32[2,16,3072]{1,0,2:T(2,128)S(1)} %copy.179, s32[1024]{0:T(1024)S(1)} %copy-done.28), kind=kCustom, calls=%fused_computation.33.clone | custom fusion | bytes 266240 | tf_op jit(solution)/shard_map/jit(_take)/gather | solution.py:35
  553.2 7.5 %gather_fusion.34 = f32[1024,2,16]{2,1,0:T(2,128)} fusion(f32[2,16,3072]{1,0,2:T(2,128)S(1)} %copy.179, s32[1024]{0:T(1024)S(1)} %fusion.115), kind=kCustom, calls=%fused_computation.34.clone | custom fusion | bytes 266240 | tf_op jit(solution)/shard_map/jit(_take)/gather | solution.py:35
  560.7 7.5 %gather_fusion.35 = f32[1024,2,16]{2,1,0:T(2,128)} fusion(f32[2,16,3072]{1,0,2:T(2,128)S(1)} %copy.179, s32[1024]{0:T(1024)S(1)} %fusion.116), kind=kCustom, calls=%fused_computation.35.clone | custom fusion | bytes 266240 | tf_op jit(solution)/shard_map/jit(_take)/gather | solution.py:35
  (194 shorter events, 118.8 us)
Async XLA Ops:
  0.7 27.7 %copy-start.35 = (pred[2048]{0:T(1024)(128)(4,1)}, pred[2048]{0:T(1024)(128)(4,1)S(1)}, u32[]{:S(2)}) copy-start(pred[2048]{0:T(1024)(128)(4,1)S(1)} %compare_and_fusion) | copy-start | bytes 6148
  16.5 17.1 %copy-start = (f32[2,16,1024]{2,1,0:T(8,128)S(1)}, f32[2,16,1024]{2,1,0:T(8,128)}, u32[]{:S(2)}) copy-start(f32[2,16,1024]{2,1,0:T(8,128)} %param.10) | copy-start | bytes 393220
  16.5 17.1 %copy-start.39 = (s32[8,1024]{1,0:T(8,128)S(1)}, s32[8,1024]{1,0:T(8,128)}, u32[]{:S(2)}) copy-start(s32[8,1024]{1,0:T(8,128)} %param.15) | copy-start | bytes 98308
  16.5 23.1 %copy-start.34 = (f32[2,8,1024]{2,1,0:T(8,128)S(1)}, f32[2,8,1024]{2,1,0:T(8,128)}, u32[]{:S(2)}) copy-start(f32[2,8,1024]{2,1,0:T(8,128)} %param.11) | copy-start | bytes 196612
  26.5 50.7 %copy-start.41 = (f32[1024]{0:T(1024)S(1)}, f32[1024]{0:T(1024)}, u32[]{:S(2)}) copy-start(f32[1024]{0:T(1024)} %param.13) | copy-start | bytes 12292
  26.6 51.9 %copy-start.40 = (f32[8,1024]{1,0:T(8,128)S(1)}, f32[8,1024]{1,0:T(8,128)}, u32[]{:S(2)}) copy-start(f32[8,1024]{1,0:T(8,128)} %param.12) | copy-start | bytes 98308
  28.5 50.6 %all-to-all-start = ((f32[2,16,8,256]{3,1,0,2:T(8,128)}), f32[2,16,8,256]{3,1,0,2:T(8,128)S(1)}, u32[]{:S(2)}, u32[]{:S(2)}) async-start(f32[2,16,8,256]{3,1,0,2:T(8,128)} %copy.120), calls=%async_computation | async-start | bytes 524288 | tf_op jit(solution)/shard_map/all_to_all | solution.py:30
  158.7 41.6 %copy-start.36 = (pred[2048]{0:T(1024)(128)(4,1)S(1)}, pred[2048]{0:T(1024)(128)(4,1)}, u32[]{:S(2)}) copy-start(pred[2048]{0:T(1024)(128)(4,1)} %copy-done.35) | copy-start | bytes 6148
  161.9 0.6 copy-start.11
  161.9 0.6 copy-start.13
  212.1 10.3 %all-to-all-start.1 = ((f32[2,16,8,256]{3,1,0,2:T(8,128)}), f32[2,16,8,256]{3,1,0,2:T(8,128)S(1)}, u32[]{:S(2)}, u32[]{:S(2)}) async-start(f32[2,16,8,256]{3,1,0,2:T(8,128)} %copy.139), calls=%async_computation.1 | async-start | bytes 524288 | tf_op jit(solution)/shard_map/all_to_all | solution.py:30
  287.9 10.4 %copy-start.9 = (f32[1024,2,16]{2,1,0:T(2,128)S(1)}, f32[1024,2,16]{2,1,0:T(2,128)}, u32[]{:S(2)}) copy-start(f32[1024,2,16]{2,1,0:T(2,128)} %gather_fusion.15) | copy-start | bytes 393220
  290.0 9.3 %copy-start.7 = (f32[1024,2,16]{2,1,0:T(2,128)S(1)}, f32[1024,2,16]{2,1,0:T(2,128)}, u32[]{:S(2)}) copy-start(f32[1024,2,16]{2,1,0:T(2,128)} %gather_fusion.16) | copy-start | bytes 393220
  292.2 7.6 %copy-start.5 = (f32[1024,2,16]{2,1,0:T(2,128)S(1)}, f32[1024,2,16]{2,1,0:T(2,128)}, u32[]{:S(2)}) copy-start(f32[1024,2,16]{2,1,0:T(2,128)} %gather_fusion.17) | copy-start | bytes 393220
  299.8 40.6 %copy-start.37 = (pred[2048]{0:T(1024)(128)(4,1)S(1)}, pred[2048]{0:T(1024)(128)(4,1)}, u32[]{:S(2)}) copy-start(pred[2048]{0:T(1024)(128)(4,1)} %copy-done.35) | copy-start | bytes 6148
  302.1 0.6 copy-start.15
  302.1 0.6 copy-start.17
  352.3 10.3 %all-to-all-start.2 = ((f32[2,16,8,256]{3,1,0,2:T(8,128)}), f32[2,16,8,256]{3,1,0,2:T(8,128)S(1)}, u32[]{:S(2)}, u32[]{:S(2)}) async-start(f32[2,16,8,256]{3,1,0,2:T(8,128)} %copy.158), calls=%async_computation.2 | async-start | bytes 524288 | tf_op jit(solution)/shard_map/all_to_all | solution.py:30
  428.1 10.4 %copy-start.10 = (f32[1024,2,16]{2,1,0:T(2,128)S(1)}, f32[1024,2,16]{2,1,0:T(2,128)}, u32[]{:S(2)}) copy-start(f32[1024,2,16]{2,1,0:T(2,128)} %gather_fusion.24) | copy-start | bytes 393220
  430.2 9.3 %copy-start.8 = (f32[1024,2,16]{2,1,0:T(2,128)S(1)}, f32[1024,2,16]{2,1,0:T(2,128)}, u32[]{:S(2)}) copy-start(f32[1024,2,16]{2,1,0:T(2,128)} %gather_fusion.25) | copy-start | bytes 393220
  432.4 7.6 %copy-start.6 = (f32[1024,2,16]{2,1,0:T(2,128)S(1)}, f32[1024,2,16]{2,1,0:T(2,128)}, u32[]{:S(2)}) copy-start(f32[1024,2,16]{2,1,0:T(2,128)} %gather_fusion.26) | copy-start | bytes 393220
  440.0 40.6 %copy-start.38 = (pred[2048]{0:T(1024)(128)(4,1)S(1)}, pred[2048]{0:T(1024)(128)(4,1)}, u32[]{:S(2)}) copy-start(pred[2048]{0:T(1024)(128)(4,1)} %copy-done.35) | copy-start | bytes 6148
  442.2 0.6 copy-start.19
  442.2 0.6 copy-start.21
  492.4 45.7 %copy-start.29 = (s32[1024]{0:T(1024)S(1)}, s32[1024]{0:T(1024)}, u32[]{:S(2)}) copy-start(s32[1024]{0:T(1024)} %fusion.113) | copy-start | bytes 12292
  492.4 10.4 %all-to-all-start.3 = ((f32[2,16,8,256]{3,1,0,2:T(8,128)}), f32[2,16,8,256]{3,1,0,2:T(8,128)S(1)}, u32[]{:S(2)}, u32[]{:S(2)}) async-start(f32[2,16,8,256]{3,1,0,2:T(8,128)} %copy.177), calls=%async_computation.3 | async-start | bytes 524288 | tf_op jit(solution)/shard_map/all_to_all | solution.py:30
  496.2 49.5 %copy-start.28 = (s32[1024]{0:T(1024)S(1)}, s32[1024]{0:T(1024)}, u32[]{:S(2)}) copy-start(s32[1024]{0:T(1024)} %fusion.114) | copy-start | bytes 12292
  568.2 6.2 %copy-start.1 = (f32[1024,2,16]{2,1,0:T(2,128)S(1)}, f32[1024,2,16]{2,1,0:T(2,128)}, u32[]{:S(2)}) copy-start(f32[1024,2,16]{2,1,0:T(2,128)} %gather_fusion.31) | copy-start | bytes 393220
  568.2 7.3 %copy-start.2 = (f32[1024,2,16]{2,1,0:T(2,128)S(1)}, f32[1024,2,16]{2,1,0:T(2,128)}, u32[]{:S(2)}) copy-start(f32[1024,2,16]{2,1,0:T(2,128)} %gather_fusion.32) | copy-start | bytes 393220
  568.2 8.4 %copy-start.3 = (f32[1024,2,16]{2,1,0:T(2,128)S(1)}, f32[1024,2,16]{2,1,0:T(2,128)}, u32[]{:S(2)}) copy-start(f32[1024,2,16]{2,1,0:T(2,128)} %gather_fusion.33) | copy-start | bytes 393220
  574.4 5.2 copy-start.30
  574.4 5.2 copy-start.31
  574.4 5.2 copy-start.32
  574.4 5.2 copy-start.33
  575.5 3.6 copy-start.4
  576.6 3.0 copy-start.20
  576.6 3.0 copy-start.22
  576.6 3.0 copy-start.23
  576.6 3.0 copy-start.24
  576.6 3.0 copy-start.25
  576.6 3.0 copy-start.26
  576.6 3.0 copy-start.27
  576.6 4.5 copy-start.12
  576.7 4.5 copy-start.14
  576.7 4.5 copy-start.16
  576.7 4.5 copy-start.18
where the time goes:
time: 585 us; the launch traced here: 582 us
  local copies, waits for them, and re-layouts  382 us (65%)
  blocking collectives  104 us (18%)
  other arithmetic  53 us (9%)
  waiting for transfers between devices  18.3 us (3%)
  starting transfers between devices  15.9 us (3%)
  matrix products  8.07 us (1%)
    gather x64, local copies, waits for them, and re-layouts, body(): jnp.take(extended, neighbours[apply_order], axis=2) - term  293 us
    psum x4, blocking collectives, body(): intersection = lax.psum(partial_intersection, 'mesh')  89.9 us
    gather x4, local copies, waits for them, and re-layouts, body(): jnp.take(term, routes.reshape(-1), axis=2).reshape(2, rows, parts, capacity)  57.7 us
    select_n x4, other arithmetic, body(): jnp.take(term, routes.reshape(-1), axis=2).reshape(2, rows, parts, capacity)  39.9 us
    all_to_all x4, waiting for transfers between devices, body(): lax.all_to_all(packed, 'mesh', split_axis=2, concat_axis=2, tiled=True)  18.3 us
    concatenate x4, local copies, waits for them, and re-layouts, body(): jnp.concatenate([term, arrived.reshape(2, rows, parts * capacity)], axis=2)  16.6 us
    all_to_all x4, starting transfers between devices, body(): lax.all_to_all(packed, 'mesh', split_axis=2, concat_axis=2, tiled=True)  15.9 us
    all_gather x1, blocking collectives, body(): full_frozen = lax.all_gather(frozen, 'band', axis=1, tiled=True)  14.2 us
  transfers between devices with their start and end apart: 4, of which 3 were waited for; matrix products, arithmetic and copies ran while one was open for 2% of the time, Pallas kernels for 0%

commit v1 on v0

--- a/solution.py
+++ b/solution.py
@@ -25,7 +25,11 @@
         partial_intersection = jnp.einsum(
             "cmp,ocjp->omj", full_frozen, paired, precision=lax.Precision.HIGHEST
         )
-        intersection = lax.psum(partial_intersection, "mesh")
+        intersection = partial_intersection
+        for hop in (1, 2, 4):
+            intersection = intersection + lax.ppermute(
+                intersection, "mesh", [(dev, dev ^ hop) for dev in range(8)]
+            )
         packed = jnp.take(term, routes.reshape(-1), axis=2).reshape(2, rows, parts, capacity)
         arrived = lax.all_to_all(packed, "mesh", split_axis=2, concat_axis=2, tiled=True)
         extended = jnp.concatenate([term, arrived.reshape(2, rows, parts * capacity)], axis=2)

time: 585 us -> 515 us (0.88)
  blocking collectives: 104 us -> 15.8 us
  starting transfers between devices: 15.9 us -> 25.2 us
  waiting for transfers between devices: 18.3 us -> 24.4 us
    psum x4 -> x0, blocking collectives: 89.9 us -> none  [body(): intersection = lax.psum(partial_intersection, 'mesh')]
    ppermute x0 -> x12, starting transfers between devices: none -> 10.4 us  [body(): lax.ppermute(intersection, 'mesh', [(dev, dev ^ hop) for dev in range(8)])]
  transfers between devices with their start and end apart: 4 -> 16, of which waited for: 3 -> 8; matrix products, arithmetic and copies ran while one was open for 2% -> 23% of each run, Pallas kernels for 0% -> 0%
where the time goes in v1:
time: 515 us; the launch traced here: 512 us
  local copies, waits for them, and re-layouts  381 us (74%)
  other arithmetic  55.1 us (11%)
  starting transfers between devices  25.2 us (5%)
  waiting for transfers between devices  24.4 us (5%)
  blocking collectives  15.8 us (3%)
  matrix products  9.01 us (2%)
    gather x64, local copies, waits for them, and re-layouts, body(): jnp.take(extended, neighbours[apply_order], axis=2) - term  295 us
    gather x4, local copies, waits for them, and re-layouts, body(): jnp.take(term, routes.reshape(-1), axis=2).reshape(2, rows, parts, capacity)  58 us
    select_n x4, other arithmetic, body(): jnp.take(term, routes.reshape(-1), axis=2).reshape(2, rows, parts, capacity)  39.9 us
    all_to_all x4, waiting for transfers between devices, body(): lax.all_to_all(packed, 'mesh', split_axis=2, concat_axis=2, tiled=True)  18.6 us
    concatenate x4, local copies, waits for them, and re-layouts, body(): jnp.concatenate([term, arrived.reshape(2, rows, parts * capacity)], axis=2)  16.6 us
    all_gather x1, blocking collectives, body(): full_frozen = lax.all_gather(frozen, 'band', axis=1, tiled=True)  15.8 us
    all_to_all x4, starting transfers between devices, body(): lax.all_to_all(packed, 'mesh', split_axis=2, concat_axis=2, tiled=True)  14.8 us
    ppermute x12, starting transfers between devices, body(): lax.ppermute(intersection, 'mesh', [(dev, dev ^ hop) for dev in range(8)])  10.4 us
  transfers between devices with their start and end apart: 16, of which 8 were waited for; matrix products, arithmetic and copies ran while one was open for 23% of the time, Pallas kernels for 0%

profile of v1, /device:TPU:0, one launch (start us, length us, event | category | flops | bytes accessed | tf_op | source)
XLA Modules:
  0.0 511.8 jit_solution(14386396467311728361)
XLA Ops:
  0.0 15.8 %all_gather.3 = f32[2,32,1024]{2,1,0:T(8,128)S(1)} all-gather(f32[2,8,1024]{2,1,0:T(8,128)} %param.11), channel_id=1, replica_groups=mesh['mesh'=8,'band'=4] {'band'}, dimensions={1}, use_global_device_ids=true | all-gather | bytes 327680 | tf_op jit(solution)/shard_map/all_gather | solution.py:20
  20.2 14.5 %gather_fusion = f32[2048,2,16]{2,1,0:T(2,128)} fusion(f32[2,16,1024]{1,0,2:T(2,128)S(1)} %copy.119, s32[2048]{0:T(1024)S(1)} %fusion.108), kind=kCustom, calls=%fused_computation.clone | custom fusion | bytes 532480 | tf_op jit(solution)/shard_map/jit(_take)/gather | solution.py:33
  34.7 10.0 %broadcast_select_fusion.3 = f32[2048,2,16]{2,1,0:T(2,128)S(1)} fusion(f32[2048,2,16]{2,1,0:T(2,128)} %gather_fusion, pred[2048]{0:T(1024)(128)(4,1)S(1)} %compare_and_fusion), kind=kLoop, calls=%fused_computation.39 | loop fusion | flops 65536 | bytes 526336 | tf_op jit(solution)/shard_map/jit(_take)/select_n | solution.py:33
  65.9 4.1 copy.122
  70.0 7.6 %gather_fusion.1 = f32[1024,2,16]{2,1,0:T(2,128)} fusion(f32[2,16,3072]{1,0,2:T(2,128)S(1)} %copy.122, s32[1024]{0:T(1024)} %fusion.109), kind=kCustom, calls=%fused_computation.1.clone | custom fusion | bytes 266240 | tf_op jit(solution)/shard_map/jit(_take)/gather | solution.py:39
  79.7 7.6 %gather_fusion.2 = f32[1024,2,16]{2,1,0:T(2,128)} fusion(f32[2,16,3072]{1,0,2:T(2,128)S(1)} %copy.122, s32[1024]{0:T(1024)} %fusion.110), kind=kCustom, calls=%fused_computation.5.clone | custom fusion | bytes 266240 | tf_op jit(solution)/shard_map/jit(_take)/gather | solution.py:39
  89.3 7.6 %gather_fusion.3 = f32[1024,2,16]{2,1,0:T(2,128)} fusion(f32[2,16,3072]{1,0,2:T(2,128)S(1)} %copy.122, s32[1024]{0:T(1024)} %fusion.111), kind=kCustom, calls=%fused_computation.6.clone | custom fusion | bytes 266240 | tf_op jit(solution)/shard_map/jit(_take)/gather | solution.py:39
  98.9 7.6 %gather_fusion.4 = f32[1024,2,16]{2,1,0:T(2,128)} fusion(f32[2,16,3072]{1,0,2:T(2,128)S(1)} %copy.122, s32[1024]{0:T(1024)} %fusion.112), kind=kCustom, calls=%fused_computation.7.clone | custom fusion | bytes 266240 | tf_op jit(solution)/shard_map/jit(_take)/gather | solution.py:39
  108.6 7.6 %gather_fusion.5 = f32[1024,2,16]{2,1,0:T(2,128)} fusion(f32[2,16,3072]{1,0,2:T(2,128)S(1)} %copy.122, s32[1024]{0:T(1024)} %fusion.113), kind=kCustom, calls=%fused_computation.8.clone | custom fusion | bytes 266240 | tf_op jit(solution)/shard_map/jit(_take)/gather | solution.py:39
  118.2 7.6 %gather_fusion.6 = f32[1024,2,16]{2,1,0:T(2,128)} fusion(f32[2,16,3072]{1,0,2:T(2,128)S(1)} %copy.122, s32[1024]{0:T(1024)} %fusion.114), kind=kCustom, calls=%fused_computation.9.clone | custom fusion | bytes 266240 | tf_op jit(solution)/shard_map/jit(_take)/gather | solution.py:39
  127.9 7.6 %gather_fusion.7 = f32[1024,2,16]{2,1,0:T(2,128)} fusion(f32[2,16,3072]{1,0,2:T(2,128)S(1)} %copy.122, s32[1024]{0:T(1024)} %fusion.115), kind=kCustom, calls=%fused_computation.10.clone | custom fusion | bytes 266240 | tf_op jit(solution)/shard_map/jit(_take)/gather | solution.py:39
  137.5 7.6 %gather_fusion.8 = f32[1024,2,16]{2,1,0:T(2,128)} fusion(f32[2,16,3072]{1,0,2:T(2,128)S(1)} %copy.122, s32[1024]{0:T(1024)} %fusion.116), kind=kCustom, calls=%fused_computation.11.clone | custom fusion | bytes 266240 | tf_op jit(solution)/shard_map/jit(_take)/gather | solution.py:39
  153.2 14.5 %gather_fusion.9 = f32[2048,2,16]{2,1,0:T(2,128)} fusion(f32[2,16,1024]{1,0,2:T(2,128)S(1)} %copy.138, s32[2048]{0:T(1024)S(1)} %fusion.108), kind=kCustom, calls=%fused_computation.2.clone | custom fusion | bytes 532480 | tf_op jit(solution)/shard_map/jit(_take)/gather | solution.py:33
  169.3 10.0 %broadcast_select_fusion.2 = f32[2048,2,16]{2,1,0:T(2,128)S(1)} fusion(f32[2048,2,16]{2,1,0:T(2,128)} %gather_fusion.9, pred[2048]{0:T(1024)(128)(4,1)S(1)} %copy-done.33), kind=kLoop, calls=%fused_computation.38 | loop fusion | flops 65536 | bytes 526336 | tf_op jit(solution)/shard_map/jit(_take)/select_n | solution.py:33
  185.4 6.0 %all-to-all-done.1 = f32[2,16,8,256]{3,1,0,2:T(8,128)S(1)} async-done(((f32[2,16,8,256]{3,1,0,2:T(8,128)}), f32[2,16,8,256]{3,1,0,2:T(8,128)S(1)}, u32[]{:S(2)}, u32[]{:S(2)}) %all-to-all-start.1) | async-done | bytes 262176 | tf_op jit(solution)/shard_map/all_to_all | solution.py:34
  192.2 4.1 copy.141
  196.4 7.6 %gather_fusion.10 = f32[1024,2,16]{2,1,0:T(2,128)} fusion(f32[2,16,3072]{1,0,2:T(2,128)S(1)} %copy.141, s32[1024]{0:T(1024)} %fusion.109), kind=kCustom, calls=%fused_computation.12.clone | custom fusion | bytes 266240 | tf_op jit(solution)/shard_map/jit(_take)/gather | solution.py:39
  204.0 7.6 %gather_fusion.11 = f32[1024,2,16]{2,1,0:T(2,128)} fusion(f32[2,16,3072]{1,0,2:T(2,128)S(1)} %copy.141, s32[1024]{0:T(1024)} %fusion.110), kind=kCustom, calls=%fused_computation.13.clone | custom fusion | bytes 266240 | tf_op jit(solution)/shard_map/jit(_take)/gather | solution.py:39
  211.6 7.6 %gather_fusion.12 = f32[1024,2,16]{2,1,0:T(2,128)} fusion(f32[2,16,3072]{1,0,2:T(2,128)S(1)} %copy.141, s32[1024]{0:T(1024)} %fusion.111), kind=kCustom, calls=%fused_computation.14.clone | custom fusion | bytes 266240 | tf_op jit(solution)/shard_map/jit(_take)/gather | solution.py:39
  219.2 7.7 %gather_fusion.13 = f32[1024,2,16]{2,1,0:T(2,128)} fusion(f32[2,16,3072]{1,0,2:T(2,128)S(1)} %copy.141, s32[1024]{0:T(1024)} %fusion.112), kind=kCustom, calls=%fused_computation.15.clone | custom fusion | bytes 266240 | tf_op jit(solution)/shard_map/jit(_take)/gather | solution.py:39
  226.9 7.6 %gather_fusion.14 = f32[1024,2,16]{2,1,0:T(2,128)} fusion(f32[2,16,3072]{1,0,2:T(2,128)S(1)} %copy.141, s32[1024]{0:T(1024)} %fusion.113), kind=kCustom, calls=%fused_computation.16.clone | custom fusion | bytes 266240 | tf_op jit(solution)/shard_map/jit(_take)/gather | solution.py:39
  234.5 7.6 %gather_fusion.15 = f32[1024,2,16]{2,1,0:T(2,128)} fusion(f32[2,16,3072]{1,0,2:T(2,128)S(1)} %copy.141, s32[1024]{0:T(1024)} %fusion.114), kind=kCustom, calls=%fused_computation.17.clone | custom fusion | bytes 266240 | tf_op jit(solution)/shard_map/jit(_take)/gather | solution.py:39
  242.1 7.6 %gather_fusion.16 = f32[1024,2,16]{2,1,0:T(2,128)} fusion(f32[2,16,3072]{1,0,2:T(2,128)S(1)} %copy.141, s32[1024]{0:T(1024)} %fusion.115), kind=kCustom, calls=%fused_computation.18.clone | custom fusion | bytes 266240 | tf_op jit(solution)/shard_map/jit(_take)/gather | solution.py:39
  249.7 7.6 %gather_fusion.17 = f32[1024,2,16]{2,1,0:T(2,128)} fusion(f32[2,16,3072]{1,0,2:T(2,128)S(1)} %copy.141, s32[1024]{0:T(1024)} %fusion.116), kind=kCustom, calls=%fused_computation.19.clone | custom fusion | bytes 266240 | tf_op jit(solution)/shard_map/jit(_take)/gather | solution.py:39
  274.3 14.5 %gather_fusion.18 = f32[2048,2,16]{2,1,0:T(2,128)} fusion(f32[2,16,1024]{1,0,2:T(2,128)S(1)} %copy.157, s32[2048]{0:T(1024)S(1)} %fusion.108), kind=kCustom, calls=%fused_computation.3.clone | custom fusion | bytes 532480 | tf_op jit(solution)/shard_map/jit(_take)/gather | solution.py:33
  289.4 10.0 %broadcast_select_fusion.1 = f32[2048,2,16]{2,1,0:T(2,128)S(1)} fusion(f32[2048,2,16]{2,1,0:T(2,128)} %gather_fusion.18, pred[2048]{0:T(1024)(128)(4,1)S(1)} %copy-done.34), kind=kLoop, calls=%fused_computation.37 | loop fusion | flops 65536 | bytes 526336 | tf_op jit(solution)/shard_map/jit(_take)/select_n | solution.py:33
  305.6 6.3 %all-to-all-done.2 = f32[2,16,8,256]{3,1,0,2:T(8,128)S(1)} async-done(((f32[2,16,8,256]{3,1,0,2:T(8,128)}), f32[2,16,8,256]{3,1,0,2:T(8,128)S(1)}, u32[]{:S(2)}, u32[]{:S(2)}) %all-to-all-start.2) | async-done | bytes 262176 | tf_op jit(solution)/shard_map/all_to_all | solution.py:34
  312.7 4.1 copy.160
  316.8 7.6 %gather_fusion.19 = f32[1024,2,16]{2,1,0:T(2,128)} fusion(f32[2,16,3072]{1,0,2:T(2,128)S(1)} %copy.160, s32[1024]{0:T(1024)} %fusion.109), kind=kCustom, calls=%fused_computation.20.clone | custom fusion | bytes 266240 | tf_op jit(solution)/shard_map/jit(_take)/gather | solution.py:39
  324.4 7.6 %gather_fusion.20 = f32[1024,2,16]{2,1,0:T(2,128)} fusion(f32[2,16,3072]{1,0,2:T(2,128)S(1)} %copy.160, s32[1024]{0:T(1024)} %fusion.110), kind=kCustom, calls=%fused_computation.21.clone | custom fusion | bytes 266240 | tf_op jit(solution)/shard_map/jit(_take)/gather | solution.py:39
  332.1 7.6 %gather_fusion.21 = f32[1024,2,16]{2,1,0:T(2,128)} fusion(f32[2,16,3072]{1,0,2:T(2,128)S(1)} %copy.160, s32[1024]{0:T(1024)} %fusion.111), kind=kCustom, calls=%fused_computation.22.clone | custom fusion | bytes 266240 | tf_op jit(solution)/shard_map/jit(_take)/gather | solution.py:39
  339.7 7.7 %gather_fusion.22 = f32[1024,2,16]{2,1,0:T(2,128)} fusion(f32[2,16,3072]{1,0,2:T(2,128)S(1)} %copy.160, s32[1024]{0:T(1024)} %fusion.112), kind=kCustom, calls=%fused_computation.23.clone | custom fusion | bytes 266240 | tf_op jit(solution)/shard_map/jit(_take)/gather | solution.py:39
  347.3 7.6 %gather_fusion.23 = f32[1024,2,16]{2,1,0:T(2,128)} fusion(f32[2,16,3072]{1,0,2:T(2,128)S(1)} %copy.160, s32[1024]{0:T(1024)} %fusion.113), kind=kCustom, calls=%fused_computation.24.clone | custom fusion | bytes 266240 | tf_op jit(solution)/shard_map/jit(_take)/gather | solution.py:39
  354.9 7.6 %gather_fusion.24 = f32[1024,2,16]{2,1,0:T(2,128)} fusion(f32[2,16,3072]{1,0,2:T(2,128)S(1)} %copy.160, s32[1024]{0:T(1024)} %fusion.114), kind=kCustom, calls=%fused_computation.25.clone | custom fusion | bytes 266240 | tf_op jit(solution)/shard_map/jit(_take)/gather | solution.py:39
  362.5 7.6 %gather_fusion.25 = f32[1024,2,16]{2,1,0:T(2,128)} fusion(f32[2,16,3072]{1,0,2:T(2,128)S(1)} %copy.160, s32[1024]{0:T(1024)} %fusion.115), kind=kCustom, calls=%fused_computation.26.clone | custom fusion | bytes 266240 | tf_op jit(solution)/shard_map/jit(_take)/gather | solution.py:39
  370.1 7.6 %gather_fusion.26 = f32[1024,2,16]{2,1,0:T(2,128)} fusion(f32[2,16,3072]{1,0,2:T(2,128)S(1)} %copy.160, s32[1024]{0:T(1024)} %fusion.116), kind=kCustom, calls=%fused_computation.27.clone | custom fusion | bytes 266240 | tf_op jit(solution)/shard_map/jit(_take)/gather | solution.py:39
  394.8 14.5 %gather_fusion.27 = f32[2048,2,16]{2,1,0:T(2,128)} fusion(f32[2,16,1024]{1,0,2:T(2,128)S(1)} %copy.176, s32[2048]{0:T(1024)S(1)} %fusion.108), kind=kCustom, calls=%fused_computation.4.clone | custom fusion | bytes 532480 | tf_op jit(solution)/shard_map/jit(_take)/gather | solution.py:33
  409.9 10.0 %broadcast_select_fusion = f32[2048,2,16]{2,1,0:T(2,128)S(1)} fusion(f32[2048,2,16]{2,1,0:T(2,128)} %gather_fusion.27, pred[2048]{0:T(1024)(128)(4,1)S(1)} %copy-done.35), kind=kLoop, calls=%fused_computation.36 | loop fusion | flops 65536 | bytes 526336 | tf_op jit(solution)/shard_map/jit(_take)/select_n | solution.py:33
  426.2 6.3 %all-to-all-done.3 = f32[2,16,8,256]{3,1,0,2:T(8,128)S(1)} async-done(((f32[2,16,8,256]{3,1,0,2:T(8,128)}), f32[2,16,8,256]{3,1,0,2:T(8,128)S(1)}, u32[]{:S(2)}, u32[]{:S(2)}) %all-to-all-start.3) | async-done | bytes 262176 | tf_op jit(solution)/shard_map/all_to_all | solution.py:34
  433.3 4.1 copy.179
  437.4 7.6 %gather_fusion.28 = f32[1024,2,16]{2,1,0:T(2,128)} fusion(f32[2,16,3072]{1,0,2:T(2,128)S(1)} %copy.179, s32[1024]{0:T(1024)} %fusion.109), kind=kCustom, calls=%fused_computation.28.clone | custom fusion | bytes 266240 | tf_op jit(solution)/shard_map/jit(_take)/gather | solution.py:39
  445.1 7.6 %gather_fusion.29 = f32[1024,2,16]{2,1,0:T(2,128)} fusion(f32[2,16,3072]{1,0,2:T(2,128)S(1)} %copy.179, s32[1024]{0:T(1024)} %fusion.110), kind=kCustom, calls=%fused_computation.29.clone | custom fusion | bytes 266240 | tf_op jit(solution)/shard_map/jit(_take)/gather | solution.py:39
  452.7 7.5 %gather_fusion.30 = f32[1024,2,16]{2,1,0:T(2,128)} fusion(f32[2,16,3072]{1,0,2:T(2,128)S(1)} %copy.179, s32[1024]{0:T(1024)S(1)} %copy-done.31), kind=kCustom, calls=%fused_computation.30.clone | custom fusion | bytes 266240 | tf_op jit(solution)/shard_map/jit(_take)/gather | solution.py:39
  460.2 7.5 %gather_fusion.31 = f32[1024,2,16]{2,1,0:T(2,128)} fusion(f32[2,16,3072]{1,0,2:T(2,128)S(1)} %copy.179, s32[1024]{0:T(1024)S(1)} %copy-done.30), kind=kCustom, calls=%fused_computation.31.clone | custom fusion | bytes 266240 | tf_op jit(solution)/shard_map/jit(_take)/gather | solution.py:39
  467.7 7.6 %gather_fusion.32 = f32[1024,2,16]{2,1,0:T(2,128)} fusion(f32[2,16,3072]{1,0,2:T(2,128)S(1)} %copy.179, s32[1024]{0:T(1024)} %fusion.113), kind=kCustom, calls=%fused_computation.32.clone | custom fusion | bytes 266240 | tf_op jit(solution)/shard_map/jit(_take)/gather | solution.py:39
  475.3 7.6 %gather_fusion.33 = f32[1024,2,16]{2,1,0:T(2,128)} fusion(f32[2,16,3072]{1,0,2:T(2,128)S(1)} %copy.179, s32[1024]{0:T(1024)} %fusion.114), kind=kCustom, calls=%fused_computation.33.clone | custom fusion | bytes 266240 | tf_op jit(solution)/shard_map/jit(_take)/gather | solution.py:39
  482.9 7.6 %gather_fusion.34 = f32[1024,2,16]{2,1,0:T(2,128)} fusion(f32[2,16,3072]{1,0,2:T(2,128)S(1)} %copy.179, s32[1024]{0:T(1024)} %fusion.115), kind=kCustom, calls=%fused_computation.34.clone | custom fusion | bytes 266240 | tf_op jit(solution)/shard_map/jit(_take)/gather | solution.py:39
  490.5 7.6 %gather_fusion.35 = f32[1024,2,16]{2,1,0:T(2,128)} fusion(f32[2,16,3072]{1,0,2:T(2,128)S(1)} %copy.179, s32[1024]{0:T(1024)} %fusion.116), kind=kCustom, calls=%fused_computation.35.clone | custom fusion | bytes 266240 | tf_op jit(solution)/shard_map/jit(_take)/gather | solution.py:39
  (220 shorter events, 118.4 us)
Async XLA Ops:
  18.0 38.9 %collective-permute-start = (f32[2,32,16]{1,2,0:T(8,128)S(1)}, f32[2,32,16]{1,2,0:T(8,128)S(1)}, u32[]{:S(2)}, u32[]{:S(2)}) collective-permute-start(f32[2,32,16]{1,2,0:T(8,128)S(1)} %convolution_bitcast_fusion.7), channel_id=1, source_target_pairs={{0,4},{4,0},{8,12},{12,8},{16,20},{20,16},{24,28},{28,24},{1,5},{5... | collective-permute-start | bytes 12296 | tf_op jit(solution)/shard_map/ppermute | solution.py:30
  20.2 26.4 %copy-start.32 = (pred[2048]{0:T(1024)(128)(4,1)}, pred[2048]{0:T(1024)(128)(4,1)S(1)}, u32[]{:S(2)}) copy-start(pred[2048]{0:T(1024)(128)(4,1)S(1)} %compare_and_fusion) | copy-start | bytes 6148
  34.7 15.7 %copy-start.36 = (s32[8,1024]{1,0:T(8,128)S(1)}, s32[8,1024]{1,0:T(8,128)}, u32[]{:S(2)}) copy-start(s32[8,1024]{1,0:T(8,128)} %param.15) | copy-start | bytes 98308
  34.7 20.4 %copy-start.37 = (f32[8,1024]{1,0:T(8,128)S(1)}, f32[8,1024]{1,0:T(8,128)}, u32[]{:S(2)}) copy-start(f32[8,1024]{1,0:T(8,128)} %param.12) | copy-start | bytes 98308
  34.7 30.4 %copy-start = (f32[2,16,1024]{2,1,0:T(8,128)S(1)}, f32[2,16,1024]{2,1,0:T(8,128)}, u32[]{:S(2)}) copy-start(f32[2,16,1024]{2,1,0:T(8,128)} %param.10) | copy-start | bytes 393220
  46.6 18.5 %all-to-all-start = ((f32[2,16,8,256]{3,1,0,2:T(8,128)}), f32[2,16,8,256]{3,1,0,2:T(8,128)S(1)}, u32[]{:S(2)}, u32[]{:S(2)}) async-start(f32[2,16,8,256]{3,1,0,2:T(8,128)} %copy.120), calls=%async_computation | async-start | bytes 524288 | tf_op jit(solution)/shard_map/all_to_all | solution.py:34
  56.9 3.8 collective-permute-start.1
  60.7 3.7 collective-permute-start.2
  145.1 7.0 %copy-start.38 = (f32[1024]{0:T(1024)S(1)}, f32[1024]{0:T(1024)}, u32[]{:S(2)}) copy-start(f32[1024]{0:T(1024)} %param.13) | copy-start | bytes 12292
  145.1 24.1 %copy-start.33 = (pred[2048]{0:T(1024)(128)(4,1)S(1)}, pred[2048]{0:T(1024)(128)(4,1)}, u32[]{:S(2)}) copy-start(pred[2048]{0:T(1024)(128)(4,1)} %copy-done.32) | copy-start | bytes 6148
  148.4 3.7 copy-start.11
  148.4 3.7 copy-start.13
  148.8 1.2 collective-permute-start.3
  150.1 17.6 %collective-permute-start.4 = (f32[2,32,16]{1,2,0:T(8,128)S(1)}, f32[2,32,16]{1,2,0:T(8,128)S(1)}, u32[]{:S(2)}, u32[]{:S(2)}) collective-permute-start(f32[2,32,16]{1,2,0:T(8,128)S(1)} %add.176), channel_id=1, source_target_pairs={{0,8},{4,12},{8,0},{12,4},{16,24},{20,28},{24,16},{28,20},{1,9},{5... | collective-permute-start | bytes 12296 | tf_op jit(solution)/shard_map/ppermute | solution.py:30
  167.7 17.0 %collective-permute-start.5 = (f32[2,32,16]{1,2,0:T(8,128)S(1)}, f32[2,32,16]{1,2,0:T(8,128)S(1)}, u32[]{:S(2)}, u32[]{:S(2)}) collective-permute-start(f32[2,32,16]{1,2,0:T(8,128)S(1)} %add.177), channel_id=1, source_target_pairs={{0,16},{4,20},{8,24},{12,28},{16,0},{20,4},{24,8},{28,12},{1,17},{... | collective-permute-start | bytes 12296 | tf_op jit(solution)/shard_map/ppermute | solution.py:30
  181.1 10.3 %all-to-all-start.1 = ((f32[2,16,8,256]{3,1,0,2:T(8,128)}), f32[2,16,8,256]{3,1,0,2:T(8,128)S(1)}, u32[]{:S(2)}, u32[]{:S(2)}) async-start(f32[2,16,8,256]{3,1,0,2:T(8,128)} %copy.139), calls=%async_computation.1 | async-start | bytes 524288 | tf_op jit(solution)/shard_map/all_to_all | solution.py:34
  257.3 10.4 %copy-start.9 = (f32[1024,2,16]{2,1,0:T(2,128)S(1)}, f32[1024,2,16]{2,1,0:T(2,128)}, u32[]{:S(2)}) copy-start(f32[1024,2,16]{2,1,0:T(2,128)} %gather_fusion.15) | copy-start | bytes 393220
  259.4 9.3 %copy-start.7 = (f32[1024,2,16]{2,1,0:T(2,128)S(1)}, f32[1024,2,16]{2,1,0:T(2,128)}, u32[]{:S(2)}) copy-start(f32[1024,2,16]{2,1,0:T(2,128)} %gather_fusion.16) | copy-start | bytes 393220
  261.5 7.6 %copy-start.5 = (f32[1024,2,16]{2,1,0:T(2,128)S(1)}, f32[1024,2,16]{2,1,0:T(2,128)}, u32[]{:S(2)}) copy-start(f32[1024,2,16]{2,1,0:T(2,128)} %gather_fusion.17) | copy-start | bytes 393220
  269.2 20.2 %copy-start.34 = (pred[2048]{0:T(1024)(128)(4,1)S(1)}, pred[2048]{0:T(1024)(128)(4,1)}, u32[]{:S(2)}) copy-start(pred[2048]{0:T(1024)(128)(4,1)} %copy-done.32) | copy-start | bytes 6148
  271.9 1.2 collective-permute-start.6
  273.2 15.6 %collective-permute-start.7 = (f32[2,32,16]{1,2,0:T(8,128)S(1)}, f32[2,32,16]{1,2,0:T(8,128)S(1)}, u32[]{:S(2)}, u32[]{:S(2)}) collective-permute-start(f32[2,32,16]{1,2,0:T(8,128)S(1)} %add.188), channel_id=1, source_target_pairs={{0,8},{4,12},{8,0},{12,4},{16,24},{20,28},{24,16},{28,20},{1,9},{5... | collective-permute-start | bytes 12296 | tf_op jit(solution)/shard_map/ppermute | solution.py:30
  288.8 16.1 %collective-permute-start.8 = (f32[2,32,16]{1,2,0:T(8,128)S(1)}, f32[2,32,16]{1,2,0:T(8,128)S(1)}, u32[]{:S(2)}, u32[]{:S(2)}) collective-permute-start(f32[2,32,16]{1,2,0:T(8,128)S(1)} %add.189), channel_id=1, source_target_pairs={{0,16},{4,20},{8,24},{12,28},{16,0},{20,4},{24,8},{28,12},{1,17},{... | collective-permute-start | bytes 12296 | tf_op jit(solution)/shard_map/ppermute | solution.py:30
  301.3 10.6 %all-to-all-start.2 = ((f32[2,16,8,256]{3,1,0,2:T(8,128)}), f32[2,16,8,256]{3,1,0,2:T(8,128)S(1)}, u32[]{:S(2)}, u32[]{:S(2)}) async-start(f32[2,16,8,256]{3,1,0,2:T(8,128)} %copy.158), calls=%async_computation.2 | async-start | bytes 524288 | tf_op jit(solution)/shard_map/all_to_all | solution.py:34
  377.8 10.4 %copy-start.10 = (f32[1024,2,16]{2,1,0:T(2,128)S(1)}, f32[1024,2,16]{2,1,0:T(2,128)}, u32[]{:S(2)}) copy-start(f32[1024,2,16]{2,1,0:T(2,128)} %gather_fusion.24) | copy-start | bytes 393220
  379.9 9.3 %copy-start.8 = (f32[1024,2,16]{2,1,0:T(2,128)S(1)}, f32[1024,2,16]{2,1,0:T(2,128)}, u32[]{:S(2)}) copy-start(f32[1024,2,16]{2,1,0:T(2,128)} %gather_fusion.25) | copy-start | bytes 393220
  382.0 7.6 %copy-start.6 = (f32[1024,2,16]{2,1,0:T(2,128)S(1)}, f32[1024,2,16]{2,1,0:T(2,128)}, u32[]{:S(2)}) copy-start(f32[1024,2,16]{2,1,0:T(2,128)} %gather_fusion.26) | copy-start | bytes 393220
  389.6 20.3 %copy-start.35 = (pred[2048]{0:T(1024)(128)(4,1)S(1)}, pred[2048]{0:T(1024)(128)(4,1)}, u32[]{:S(2)}) copy-start(pred[2048]{0:T(1024)(128)(4,1)} %copy-done.32) | copy-start | bytes 6148
  392.4 1.2 collective-permute-start.9
  393.6 15.6 %collective-permute-start.10 = (f32[2,32,16]{1,2,0:T(8,128)S(1)}, f32[2,32,16]{1,2,0:T(8,128)S(1)}, u32[]{:S(2)}, u32[]{:S(2)}) collective-permute-start(f32[2,32,16]{1,2,0:T(8,128)S(1)} %add.200), channel_id=1, source_target_pairs={{0,8},{4,12},{8,0},{12,4},{16,24},{20,28},{24,16},{28,20},{1,9},{5... | collective-permute-start | bytes 12296 | tf_op jit(solution)/shard_map/ppermute | solution.py:30
  409.3 16.3 %collective-permute-start.11 = (f32[2,32,16]{1,2,0:T(8,128)S(1)}, f32[2,32,16]{1,2,0:T(8,128)S(1)}, u32[]{:S(2)}, u32[]{:S(2)}) collective-permute-start(f32[2,32,16]{1,2,0:T(8,128)S(1)} %add.201), channel_id=1, source_target_pairs={{0,16},{4,20},{8,24},{12,28},{16,0},{20,4},{24,8},{28,12},{1,17},{... | collective-permute-start | bytes 12296 | tf_op jit(solution)/shard_map/ppermute | solution.py:30
  421.8 30.9 %copy-start.31 = (s32[1024]{0:T(1024)S(1)}, s32[1024]{0:T(1024)}, u32[]{:S(2)}) copy-start(s32[1024]{0:T(1024)} %fusion.111) | copy-start | bytes 12292
  421.8 38.5 %copy-start.30 = (s32[1024]{0:T(1024)S(1)}, s32[1024]{0:T(1024)}, u32[]{:S(2)}) copy-start(s32[1024]{0:T(1024)} %fusion.112) | copy-start | bytes 12292
  421.8 10.7 %all-to-all-start.3 = ((f32[2,16,8,256]{3,1,0,2:T(8,128)}), f32[2,16,8,256]{3,1,0,2:T(8,128)S(1)}, u32[]{:S(2)}, u32[]{:S(2)}) async-start(f32[2,16,8,256]{3,1,0,2:T(8,128)} %copy.177), calls=%async_computation.3 | async-start | bytes 524288 | tf_op jit(solution)/shard_map/all_to_all | solution.py:34
  498.1 6.2 %copy-start.1 = (f32[1024,2,16]{2,1,0:T(2,128)S(1)}, f32[1024,2,16]{2,1,0:T(2,128)}, u32[]{:S(2)}) copy-start(f32[1024,2,16]{2,1,0:T(2,128)} %gather_fusion.31) | copy-start | bytes 393220
  498.1 7.3 %copy-start.2 = (f32[1024,2,16]{2,1,0:T(2,128)S(1)}, f32[1024,2,16]{2,1,0:T(2,128)}, u32[]{:S(2)}) copy-start(f32[1024,2,16]{2,1,0:T(2,128)} %gather_fusion.32) | copy-start | bytes 393220
  498.1 8.4 %copy-start.3 = (f32[1024,2,16]{2,1,0:T(2,128)S(1)}, f32[1024,2,16]{2,1,0:T(2,128)}, u32[]{:S(2)}) copy-start(f32[1024,2,16]{2,1,0:T(2,128)} %gather_fusion.33) | copy-start | bytes 393220
  504.4 5.1 copy-start.28
  504.4 5.1 %copy-start.29 = (f32[1,1024]{1,0:T(1,128)S(1)}, f32[1,1024]{1,0:T(1,128)}, u32[]{:S(2)}) copy-start(f32[1,1024]{1,0:T(1,128)} %get-tuple-element.32) | copy-start | bytes 12292
  505.4 3.6 copy-start.4
  506.5 3.0 copy-start.24
  506.5 3.0 copy-start.25
  506.5 3.0 copy-start.26
  506.5 3.0 copy-start.27
  506.5 4.5 copy-start.12
  506.5 4.5 copy-start.14
  506.6 4.5 copy-start.16
  506.6 4.5 copy-start.18
  (7 other events, 15.8 us)
